TPU v7x, 512 devices: a whole 4x4x16 slice. The times are simulated.
512 devices in a mesh: fsdp: 32 (over x, z_hi, core), ctx: 16 (over y, z_lo).
Axes of the slice: x: 4, y: 4, z: 16 (z_hi: 4, z_lo: 4; z = z_hi * 4 + z_lo), core: 2. Of those that a mesh axis runs over, the one named last changes fastest.
Arguments:
- features: bfloat16 [3, 16384, 8192], P(None, 'ctx', 'fsdp'), may hold values from -6 to 6
- short_taps: float32 [3, 3, 8192], P(None, None, 'fsdp'), may hold values from -3.5 to 3.5
- decay_rates: float32 [512, 16], P('fsdp'), may hold values from 1.5258789e-05 to 0.1
- mode_gains: float32 [512, 16], P('fsdp'), may hold values from -2.5 to 2.5
- cotangent: bfloat16 [16384, 8192], P('ctx', 'fsdp'), may hold values from -6 to 6
Outputs:
- mixer_output: bfloat16 [16384, 8192], P('ctx', 'fsdp')
- feature_grads: bfloat16 [3, 16384, 8192], P(None, 'ctx', 'fsdp')
- gain_grads: float32 [512, 16], P('fsdp')
- rate_grads: float32 [512, 16], P('fsdp')
All inputs are finite; a program needn't handle non-finite values.
Results may differ from a plain program's by a relative error of at most 0.0048.
Values may be sent and summed in bfloat16 or wider, within the bound.
A program may use at most 64 MiB of HBM per device.

v0:
```python
import jax
import jax.numpy as jnp
from jax import lax
from jax.sharding import PartitionSpec as P

precise = lax.Precision.HIGHEST
threepass = lax.Precision.HIGH


def passed_along(value, axis, steps):
    count = lax.axis_size(axis)
    leading, last = (max(0, -steps), min(count, count - steps))
    return lax.ppermute(value, axis, [(source, source + steps) for source in range(leading, last)])


def diagonal_sums(gram_acc):
    group_count, block_len, width_same = gram_acc.shape
    flipped = jnp.flip(gram_acc, axis=2)
    padded = jnp.concatenate([flipped, jnp.zeros_like(flipped)], axis=2)
    flattened = padded.reshape(group_count, 2 * block_len * block_len)[
        :, : block_len * (2 * block_len - 1)
    ]
    sheared = flattened.reshape(group_count, block_len, 2 * block_len - 1)
    return jnp.sum(sheared, axis=1)[:, block_len - 1 :]


def short_conv(taps_table, row_data, tokens, rim_rows, forward):
    summed = jnp.zeros((3, tokens, row_data.shape[2]), jnp.float32)
    for offset in range(taps_table.shape[1]):
        start_row = rim_rows - offset if forward else offset
        summed = (
            summed + taps_table[:, offset, None, :] * row_data[:, start_row : start_row + tokens, :]
        )
    return summed


def per_device(features, short_taps, decay_rates, mode_gains, cotangent):
    tokens = features.shape[1]
    channels = features.shape[2]
    group_count = decay_rates.shape[0]
    order_count = decay_rates.shape[1]
    members = channels // group_count
    rim_rows = short_taps.shape[1] - 1
    block_len = 128
    block_count = tokens // block_len
    ctx_count = lax.axis_size("ctx")
    ctx_index = lax.axis_index("ctx")
    earlier_rows = passed_along(features[:, tokens - rim_rows :, :], "ctx", 1)
    extended = jnp.concatenate([earlier_rows, features], axis=1)
    shaped = short_conv(short_taps, extended, tokens, rim_rows, True)
    query_part, key_part, value_part = (shaped[0], shaped[1], shaped[2])
    product = (key_part * value_part).astype(jnp.bfloat16)
    adjoint = cotangent * query_part
    grouped_z = product.reshape(tokens, group_count, members)
    grouped_e = adjoint.reshape(tokens, group_count, members)
    mode_coefs = mode_gains * jnp.sqrt(2.0 * decay_rates)
    rate_axis = decay_rates[:, :, None]
    positions = jnp.arange(tokens, dtype=jnp.float32)[None, None, :]
    decay_from = jnp.exp(-rate_axis * positions)
    end_tables = jnp.stack([jnp.flip(decay_from, 2), -jnp.flip(positions * decay_from, 2)])
    end_states = jnp.einsum(
        "kgns,sgm->kngm", end_tables, grouped_z.astype(jnp.float32), precision=threepass
    )
    start_state = jnp.einsum("gnt,tgm->ngm", decay_from, grouped_e, precision=precise)
    local_states = jnp.stack([end_states[0], end_states[1], start_state]).reshape(
        3, order_count, channels
    )
    rate_cols = jnp.repeat(decay_rates.T, members, axis=1)
    everyone = lax.all_gather(local_states[None], "ctx", axis=0, tiled=True)
    device_ids = jnp.arange(ctx_count, dtype=jnp.int32)
    ahead_steps = (ctx_index - 1 - device_ids).astype(jnp.float32)[:, None, None]
    behind_steps = (device_ids - ctx_index - 1).astype(jnp.float32)[:, None, None]
    ahead_weight = jnp.where(
        ahead_steps >= 0, jnp.exp(-rate_cols[None] * (tokens * jnp.maximum(ahead_steps, 0.0))), 0.0
    )
    behind_weight = jnp.where(
        behind_steps >= 0,
        jnp.exp(-rate_cols[None] * (tokens * jnp.maximum(behind_steps, 0.0))),
        0.0,
    )
    prev_state = jnp.sum(ahead_weight * everyone[:, 0], axis=0)
    prev_lagged = jnp.sum(
        ahead_weight * (everyone[:, 1] - tokens * ahead_steps * everyone[:, 0]), axis=0
    )
    next_state = jnp.sum(behind_weight * everyone[:, 2], axis=0)
    lag_axis = jnp.arange(block_len, dtype=jnp.float32)[None, None, :]
    block_pow = jnp.exp(-rate_axis * lag_axis)
    block_after = block_pow * jnp.exp(-rate_axis)
    block_moments = jnp.stack([block_after, (lag_axis + 1.0) * block_after])
    coef_after = mode_coefs[:, :, None] * block_after
    block_ends = jnp.stack([jnp.flip(block_pow, 2), -jnp.flip(lag_axis * block_pow, 2)])
    coef_tail = mode_coefs[:, :, None] * jnp.flip(block_after, 2)
    block_span = jnp.exp(-decay_rates * block_len).T[:, :, None]
    filter_taps = jnp.sum(mode_coefs[:, :, None] * block_pow, axis=1)
    lag_index = (
        jnp.arange(block_len, dtype=jnp.int32)[:, None]
        - jnp.arange(block_len, dtype=jnp.int32)[None, :]
    )
    toeplitz = jnp.where(lag_index[None] >= 0, filter_taps[:, jnp.maximum(lag_index, 0)], 0.0)
    z_blocks = grouped_z.reshape(block_count, block_len, group_count, members)
    e_blocks = grouped_e.reshape(block_count, block_len, group_count, members)

    def forward_block(carried_in, inputs):
        mode_state, lagged, first_acc, lag_acc, gram_acc = carried_in
        z_block, e_block = inputs
        z_wide = z_block.astype(jnp.float32)
        inside_part = jnp.einsum("gts,sgm->tgm", toeplitz, z_wide, precision=threepass)
        carried = jnp.einsum("gnt,ngm->tgm", coef_after, mode_state, precision=precise)
        moments = jnp.einsum("kgnt,tgm->kngm", block_moments, e_block, precision=precise)
        first_acc = first_acc + jnp.sum(moments[0] * mode_state, axis=2)
        lag_acc = lag_acc + jnp.sum(moments[0] * lagged - moments[1] * mode_state, axis=2)
        gram_acc = gram_acc + jnp.einsum("tgm,sgm->gts", e_block, z_wide, precision=precise)
        fresh_part = jnp.einsum("kgns,sgm->kngm", block_ends, z_wide, precision=threepass)
        new_lagged = block_span * lagged - block_len * block_span * mode_state + fresh_part[1]
        new_state = block_span * mode_state + fresh_part[0]
        return ((new_state, new_lagged, first_acc, lag_acc, gram_acc), inside_part + carried)

    zero_state = jnp.zeros((order_count, group_count, members), jnp.float32)
    zero_pairs = jnp.zeros((order_count, group_count), jnp.float32)
    zero_gram = jnp.zeros((group_count, block_len, block_len), jnp.float32)
    final_carry, inner_blocks = lax.scan(
        forward_block,
        (zero_state, zero_state, zero_pairs, zero_pairs, zero_gram),
        (z_blocks, e_blocks),
    )
    first_acc, lag_acc, gram_acc = (final_carry[2], final_carry[3], final_carry[4])

    def backward_block(later_state, e_block):
        inside_part = jnp.einsum("gts,tgm->sgm", toeplitz, e_block, precision=precise)
        carried = jnp.einsum("gns,ngm->sgm", coef_tail, later_state, precision=precise)
        fresh_part = jnp.einsum("gnt,tgm->ngm", block_pow, e_block, precision=precise)
        return (block_span * later_state + fresh_part, inside_part + carried)

    top_state, grad_blocks = lax.scan(backward_block, zero_state, e_blocks, reverse=True)
    prev_grouped = prev_state.reshape(order_count, group_count, members)
    lagged_grouped = prev_lagged.reshape(order_count, group_count, members)
    next_grouped = next_state.reshape(order_count, group_count, members)
    device_after = decay_from * jnp.exp(-rate_axis)
    inner_sum = inner_blocks.reshape(tokens, group_count, members) + jnp.einsum(
        "gnt,ngm->tgm", mode_coefs[:, :, None] * device_after, prev_grouped, precision=precise
    )
    first_moment = jnp.exp(-decay_rates).T[:, :, None] * start_state
    second_moment = jnp.einsum(
        "gnt,tgm->ngm", (positions + 1.0) * device_after, grouped_e, precision=precise
    )
    first_acc = first_acc + jnp.sum(first_moment * prev_grouped, axis=2)
    lag_acc = lag_acc + jnp.sum(
        first_moment * lagged_grouped - second_moment * prev_grouped, axis=2
    )
    device_tail = mode_coefs[:, :, None] * jnp.flip(device_after, 2)
    product_grad = grad_blocks.reshape(tokens, group_count, members) + jnp.einsum(
        "gns,ngm->sgm", device_tail, next_grouped, precision=precise
    )
    lag_totals = diagonal_sums(gram_acc)
    first_total = first_acc.T + jnp.sum(lag_totals[:, None, :] * block_pow, axis=2)
    lag_total = lag_acc.T - jnp.sum(lag_totals[:, None, :] * lag_axis * block_pow, axis=2)
    gain_part = jnp.sqrt(2.0 * decay_rates) * first_total
    rate_part = mode_coefs * (0.5 * first_total + decay_rates * lag_total)
    inner_flat = inner_sum.reshape(tokens, channels)
    mixer_output = (query_part * inner_flat).astype(jnp.bfloat16)
    grad_flat = product_grad.reshape(tokens, channels)
    feature_adj = jnp.stack([cotangent * inner_flat, grad_flat * value_part, grad_flat * key_part])
    later_rows = passed_along(feature_adj[:, :rim_rows, :], "ctx", -1)
    appended = jnp.concatenate([feature_adj, later_rows], axis=1)
    feature_grads = short_conv(short_taps, appended, tokens, rim_rows, False).astype(jnp.bfloat16)
    filter_local = jnp.stack([gain_part, rate_part])
    entry_count = 2 * group_count * order_count * lax.axis_size("fsdp")
    summed = lax.psum(filter_local, "ctx")
    squares = lax.psum(jnp.sum(summed * summed), "fsdp")
    factor = jnp.minimum(1.0, lax.rsqrt(squares / entry_count + 1e-06))
    clipped = summed * factor
    return (mixer_output, feature_grads, clipped[0], clipped[1])


def solution(mesh):
    return jax.shard_map(
        per_device,
        mesh=mesh,
        in_specs=(
            P(None, "ctx", "fsdp"),
            P(None, None, "fsdp"),
            P("fsdp", None),
            P("fsdp", None),
            P("ctx", "fsdp"),
        ),
        out_specs=(P("ctx", "fsdp"), P(None, "ctx", "fsdp"), P("fsdp", None), P("fsdp", None)),
        check_vma=False,
    )
```

profile of v0, /device:TPU:1, one launch (start us, length us, event | category | flops | bytes accessed | tf_op | source)
XLA Modules:
  0.0 575.3 jit_solution(6784911890546579179)
XLA Ops:
  2.2 5.1 collective-permute-start
  14.9 54.5 %gather_fusion = f32[16384,16]{1,0:T(8,128)} fusion(f32[16,128]{0,1:T(8,128)S(1)} %copy.59, s32[16384]{0:T(1024)S(1)} %bitcast_clamp_fusion), kind=kCustom, calls=%fused_computation | custom fusion | bytes 2162688 | tf_op jit(solution)/shard_map/gather | solution.py:99
  69.4 5.2 copy.60
  77.4 2.6 copy.55
  80.0 3.3 rev.26
  87.9 4.8 multiply_add_fusion
  95.4 3.3 fusion.63
  105.0 41.3 %all_gather.3 = f32[16,3,16,256]{3,2,1,0:T(8,128)S(1)} all-gather(f32[1,3,16,256]{3,2,1,0:T(8,128)S(1)} %pad_maximum_fusion.5), channel_id=1, replica_groups=mesh['fsdp'=32,'ctx'=16] {'ctx'}, dimensions={0}, use_global_device_ids=true | all-gather | bytes 835584 | tf_op jit(solution)/shard_map/all_gather | solution.py:69
  154.0 132.3 %while.38 = (s32[]{:T(128)}, f32[16,16,16]{0,2,1:T(8,128)S(1)}, f32[16,16,16]{0,2,1:T(8,128)}, f32[16,16]{0,1:T(8,128)}, f32[16,16]{0,1:T(8,128)}, /*index=5*/f3...) while((s32[]{:T(128)}, f32[16,16,16]{0,2,1:T(8,128)S(1)}, ...), condition=%wide.region_4.5_spmd.clone, body=%wide.region_1.0_spmd.clone.sunk | while | flops 101380864 | bytes 5014714 | solution.py:121
  156.8 2.9 convolution_bitcast_fusion.8
  162.6 4.5 dynamic_update_slice.17
  172.0 2.9 convolution_bitcast_fusion.8
  179.4 4.5 dynamic_update_slice.17
  188.7 2.9 convolution_bitcast_fusion.8
  196.1 4.5 dynamic_update_slice.17
  205.5 2.9 convolution_bitcast_fusion.8
  212.9 4.5 dynamic_update_slice.17
  222.2 2.9 convolution_bitcast_fusion.8
  229.6 4.5 dynamic_update_slice.17
  239.0 2.9 convolution_bitcast_fusion.8
  246.3 4.5 dynamic_update_slice.17
  255.7 2.9 convolution_bitcast_fusion.8
  263.1 4.5 dynamic_update_slice.17
  272.5 2.9 convolution_bitcast_fusion.8
  279.8 4.5 dynamic_update_slice.17
  286.4 5.8 %rev.30 = f32[16,128,128]{2,1,0:T(8,128)} reverse(f32[16,128,128]{2,1,0:T(8,128)S(1)} %get-tuple-element.242), dimensions={2} | reverse | bytes 2097152 | tf_op jit(solution)/shard_map/jit(_flip)/rev | solution.py:18
  296.3 6.3 %reshape.172 = f32[16,128,255]{2,1,0:T(8,128)} reshape(f32[16,32640]{1,0:T(8,128)} %slice.116) | data formatting | bytes 4177920 | tf_op jit(solution)/shard_map/reshape | solution.py:23
  302.6 2.4 reduce_sum.112
  307.9 2.6 fusion.68
  311.3 61.1 %psum.14 = f32[2,16,16]{2,1,0:T(8,128)S(1)} all-reduce(f32[2,16,16]{2,1,0:T(8,128)S(1)} %pad_maximum_fusion.6), channel_id=1, replica_groups=mesh['fsdp'=32,'ctx'=16] {'ctx'}, use_global_device_ids=true, to_apply=%region_15.16 | all-reduce | flops 512 | bytes 4096 | tf_op jit(solution)/shard_map/psum | solution.py:168
  373.0 5.5 rev.29
  378.5 108.7 %psum.15 = f32[]{:T(128)} all-reduce(f32[]{:T(128)} %multiply_reduce_fusion.6), channel_id=1, replica_groups=mesh['fsdp'=32,'ctx'=16] {'fsdp'}, use_global_device_ids=true, to_apply=%region_17.18 | all-reduce | flops 1 | bytes 8 | tf_op jit(solution)/shard_map/psum | solution.py:169
  491.4 49.0 %while.39 = (s32[]{:T(128)}, f32[16,16,16]{0,2,1:T(8,128)S(1)}, f32[8,128,16,16]{1,0,3,2:T(8,128)}, f32[16,16,1]{0,1,2:T(8,128)S(1)}, f32[8,128,16,16]{1,3,2,0:T...) while((s32[]{:T(128)}, f32[16,16,16]{0,2,1:T(8,128)S(1)}, ...), condition=%wide.region_7.8_spmd.clone, body=%wide.region_6.7_spmd.clone.sunk | while | flops 62996484 | bytes 2277520 | solution.py:134
  492.6 4.5 dynamic_update_slice.18
  498.8 4.5 dynamic_update_slice.18
  504.9 4.5 dynamic_update_slice.18
  511.0 4.5 dynamic_update_slice.18
  517.2 4.5 dynamic_update_slice.18
  523.3 4.5 dynamic_update_slice.18
  529.4 4.5 dynamic_update_slice.18
  535.5 4.5 dynamic_update_slice.18
  540.4 2.5 reshape.168
  543.0 2.6 fusion.61
  547.3 2.4 reshape.164
  549.6 2.6 fusion.62
  558.4 9.5 %collective-permute-done.1 = f32[3,2,256]{1,2,0:T(8,128)S(1)} collective-permute-done((f32[3,2,256]{1,2,0:T(8,128)S(1)}, f32[3,2,256]{1,2,0:T(8,128)S(1)}, u32[]{:S(2)}, u32[]{:S(2)}) %collective-permute-start.1) | collective-permute-done | bytes 6176 | tf_op jit(solution)/shard_map/ppermute | solution.py:13
  569.5 3.3 fusion.54
  572.8 2.6 copy.77
  (215 shorter events, 140.8 us)
Async XLA Ops:
  2.2 85.7 %collective-permute-start = (bf16[3,2,256]{1,2,0:T(8,128)(2,1)}, bf16[3,2,256]{1,2,0:T(8,128)(2,1)}, u32[]{:S(2)}, u32[]{:S(2)}) collective-permute-start(bf16[3,2,256]{1,2,0:T(8,128)(2,1)} %copy.56), channel_id=1, source_target_pairs={{0,1},{1,2},{2,3},{3,4},{4,5},{5,6},{6,7},{7,8},{8,9},{9,10},{10,1... | collective-permute-start | bytes 9224 | tf_op jit(solution)/shard_map/ppermute | solution.py:13
  10.3 4.0 copy-start.19
  10.3 4.3 copy-start.17
  10.3 3.4 copy-start.29
  76.7 6.5 %copy-start.28 = (f32[3,1,256]{2,1,0:T(1,128)S(1)}, f32[3,1,256]{2,1,0:T(1,128)}, u32[]{:S(2)}) copy-start(f32[3,1,256]{2,1,0:T(1,128)} %get-tuple-element.483) | copy-start | bytes 9220
  77.4 7.9 %copy-start.27 = (f32[16,16]{0,1:T(8,128)S(1)}, f32[16,16]{0,1:T(8,128)}, u32[]{:S(2)}) copy-start(f32[16,16]{0,1:T(8,128)} %get-tuple-element.489) | copy-start | bytes 3076
  83.2 4.6 copy-start.25
  92.7 1.6 copy-start
  92.7 2.6 copy-start.10
  92.7 2.7 copy-start.11
  102.1 49.1 %copy-start.8 = (f32[1024,256]{0,1:T(8,128)}, f32[1024,256]{0,1:T(8,128)S(1)}, u32[]{:S(2)}) copy-start(f32[1024,256]{0,1:T(8,128)S(1)} %convert_multiply_fusion.1) | copy-start | bytes 3145732
  103.6 47.8 %copy-start.15 = (f32[16,16,16]{2,1,0:T(8,128)}, f32[16,16,16]{2,1,0:T(8,128)S(1)}, u32[]{:S(2)}) copy-start(f32[16,16,16]{2,1,0:T(8,128)S(1)} %fusion.75) | copy-start | bytes 49156
  150.9 1.0 copy-start.12
  296.3 10.9 %copy-start.14 = (f32[16,256]{0,1:T(8,128)S(1)}, f32[16,256]{0,1:T(8,128)}, u32[]{:S(2)}) copy-start(f32[16,256]{0,1:T(8,128)} %copy.70) | copy-start | bytes 49156
  296.3 10.9 %copy-start.16 = (f32[16,16,16]{2,1,0:T(8,128)S(1)}, f32[16,16,16]{2,1,0:T(8,128)}, u32[]{:S(2)}) copy-start(f32[16,16,16]{2,1,0:T(8,128)} %copy-done.15) | copy-start | bytes 49156
  296.3 11.6 %copy-start.9 = (f32[1024,256]{0,1:T(8,128)S(1)}, f32[1024,256]{0,1:T(8,128)}, u32[]{:S(2)}) copy-start(f32[1024,256]{0,1:T(8,128)} %copy-done.8) | copy-start | bytes 3145732
  491.4 51.5 %copy-start.21 = (f32[16,256]{1,0:T(8,128)S(1)}, f32[16,256]{1,0:T(8,128)}, u32[]{:S(2)}) copy-start(f32[16,256]{1,0:T(8,128)} %get-tuple-element.414) | copy-start | bytes 49156
  491.4 51.6 %copy-start.20 = (f32[16,16]{1,0:T(8,128)S(1)}, f32[16,16]{1,0:T(8,128)}, u32[]{:S(2)}) copy-start(f32[16,16]{1,0:T(8,128)} %get-tuple-element.758) | copy-start | bytes 3076
  540.4 5.2 copy-start.1
  545.6 4.0 copy-start.18
  549.6 4.6 copy-start.2
  549.6 4.6 copy-start.4
  554.3 1.0 copy-start.6
  554.3 2.5 copy-start.22
  554.3 3.1 copy-start.13
  554.3 13.6 %copy-start.3 = (f32[1,1024,256]{1,2,0:T(8,128)S(1)}, f32[1,1024,256]{1,2,0:T(8,128)}, u32[]{:S(2)}) copy-start(f32[1,1024,256]{1,2,0:T(8,128)} %get-tuple-element.471) | copy-start | bytes 3145732
  554.3 13.6 %copy-start.5 = (f32[1,1024,256]{1,2,0:T(8,128)S(1)}, f32[1,1024,256]{1,2,0:T(8,128)}, u32[]{:S(2)}) copy-start(f32[1,1024,256]{1,2,0:T(8,128)} %get-tuple-element.472) | copy-start | bytes 3145732
  555.4 12.6 %collective-permute-start.1 = (f32[3,2,256]{1,2,0:T(8,128)S(1)}, f32[3,2,256]{1,2,0:T(8,128)S(1)}, u32[]{:S(2)}, u32[]{:S(2)}) collective-permute-start(f32[3,2,256]{1,2,0:T(8,128)S(1)} %slice.113), channel_id=1, source_target_pairs={{1,0},{2,1},{3,2},{4,3},{5,4},{6,5},{7,6},{8,7},{9,8},{10,9},{11,1... | collective-permute-start | bytes 18440 | tf_op jit(solution)/shard_map/ppermute | solution.py:13
  558.4 11.0 %copy-start.7 = (f32[1,1024,256]{1,2,0:T(8,128)S(1)}, f32[1,1024,256]{1,2,0:T(8,128)}, u32[]{:S(2)}) copy-start(f32[1,1024,256]{1,2,0:T(8,128)} %copy-done.6) | copy-start | bytes 3145732
  558.4 11.0 %copy-start.23 = (f32[3,256]{1,0:T(4,128)S(1)}, f32[3,256]{1,0:T(4,128)}, u32[]{:S(2)}) copy-start(f32[3,256]{1,0:T(4,128)} %get-tuple-element.499) | copy-start | bytes 9220
  558.4 11.0 %copy-start.24 = (f32[3,256]{1,0:T(4,128)S(1)}, f32[3,256]{1,0:T(4,128)}, u32[]{:S(2)}) copy-start(f32[3,256]{1,0:T(4,128)} %get-tuple-element.500) | copy-start | bytes 9220
  558.4 11.0 %copy-start.26 = (f32[3,1,256]{2,0,1:T(4,128)S(1)}, f32[3,1,256]{2,0,1:T(4,128)}, u32[]{:S(2)}) copy-start(f32[3,1,256]{2,0,1:T(4,128)} %copy-done.25) | copy-start | bytes 9220
where the time goes:
time: 580 us; the launch traced here: 575 us
  blocking collectives  211 us (36%)
  local copies, waits for them, and re-layouts  189 us (33%)
  matrix products  99.5 us (17%)
  other arithmetic  57.1 us (10%)
  waiting for transfers between devices  9.53 us (2%)
  starting transfers between devices  6.47 us (1%)
    psum x1, blocking collectives, per_device(): squares = lax.psum(jnp.sum(summed * summed), 'fsdp')  109 us
    dynamic_update_slice x16, local copies, waits for them, and re-layouts, per_device(): lax.scan(forward_block, (zero_state, zero_state, zero_pairs, zero_pairs,...  71.3 us
    psum x1, blocking collectives, per_device(): summed = lax.psum(filter_local, 'ctx')  61.1 us
    gather x2, local copies, waits for them, and re-layouts, per_device(): filter_taps[:, jnp.maximum(lag_index, 0)]  59.7 us
    all_gather x1, blocking collectives, per_device(): everyone = lax.all_gather(local_states[None], 'ctx', axis=0, tiled=True)  41.3 us
    dot_general x8, matrix products, forward_block(): jnp.einsum('kgnt,tgm->kngm', block_moments, e_block, precision=precise)  23.1 us
    dot_general x8, matrix products, forward_block(): jnp.einsum('tgm,sgm->gts', e_block, z_wide, precision=precise)  16.3 us
    unnamed x72, local copies, waits for them, and re-layouts  15.9 us
  transfers between devices with their start and end apart: 2, of which 1 were waited for; matrix products, arithmetic and copies ran while one was open for 14% of the time, Pallas kernels for 0%

commit v1 on v0

--- a/solution.py
+++ b/solution.py
@@ -165,7 +165,7 @@
     feature_grads = short_conv(short_taps, appended, tokens, rim_rows, False).astype(jnp.bfloat16)
     filter_local = jnp.stack([gain_part, rate_part])
     entry_count = 2 * group_count * order_count * lax.axis_size("fsdp")
-    summed = lax.psum(filter_local, "ctx")
+    summed = jnp.sum(lax.all_gather(filter_local, "ctx"), axis=0)
     squares = lax.psum(jnp.sum(summed * summed), "fsdp")
     factor = jnp.minimum(1.0, lax.rsqrt(squares / entry_count + 1e-06))
     clipped = summed * factor

time: 580 us -> 544 us (0.938)
  blocking collectives: 211 us -> 175 us
    psum x1 -> x0, blocking collectives: 61.1 us -> none  [per_device(): summed = lax.psum(filter_local, 'ctx')]
    all_gather x0 -> x1, blocking collectives: none -> 32.1 us  [per_device(): summed = jnp.sum(lax.all_gather(filter_local, 'ctx'), axis=0)]
    psum x1, blocking collectives: 109 us -> 102 us  [per_device(): squares = lax.psum(jnp.sum(summed * summed), 'fsdp')]
    unnamed x72 -> x77, local copies, waits for them, and re-layouts: 15.9 us -> 17.3 us
  transfers between devices with their start and end apart: 2 -> 2, of which waited for: 1 -> 1; matrix products, arithmetic and copies ran while one was open for 14% -> 15% of each run, Pallas kernels for 0% -> 0%
where the time goes in v1:
time: 544 us; the launch traced here: 540 us
  local copies, waits for them, and re-layouts  190 us (35%)
  blocking collectives  175 us (32%)
  matrix products  99.5 us (18%)
  other arithmetic  56.3 us (10%)
  waiting for transfers between devices  9.4 us (2%)
  starting transfers between devices  6.47 us (1%)
    psum x1, blocking collectives, per_device(): squares = lax.psum(jnp.sum(summed * summed), 'fsdp')  102 us
    dynamic_update_slice x16, local copies, waits for them, and re-layouts, per_device(): lax.scan(forward_block, (zero_state, zero_state, zero_pairs, zero_pairs,...  71.3 us
    gather x2, local copies, waits for them, and re-layouts, per_device(): filter_taps[:, jnp.maximum(lag_index, 0)]  60 us
    all_gather x1, blocking collectives, per_device(): everyone = lax.all_gather(local_states[None], 'ctx', axis=0, tiled=True)  41.3 us
    all_gather x1, blocking collectives, per_device(): summed = jnp.sum(lax.all_gather(filter_local, 'ctx'), axis=0)  32.1 us
    dot_general x8, matrix products, forward_block(): jnp.einsum('kgnt,tgm->kngm', block_moments, e_block, precision=precise)  23.1 us
    unnamed x77, local copies, waits for them, and re-layouts  17.3 us
    dot_general x8, matrix products, forward_block(): jnp.einsum('tgm,sgm->gts', e_block, z_wide, precision=precise)  16.3 us
  transfers between devices with their start and end apart: 2, of which 1 were waited for; matrix products, arithmetic and copies ran while one was open for 15% of the time, Pallas kernels for 0%

profile of v1, /device:TPU:1, one launch (start us, length us, event | category | flops | bytes accessed | tf_op | source)
XLA Modules:
  0.0 539.8 jit_solution(11838689247109927772)
XLA Ops:
  2.2 5.0 collective-permute-start
  14.9 54.8 %gather_fusion = f32[16384,16]{1,0:T(8,128)} fusion(f32[16,128]{0,1:T(8,128)S(1)} %copy.67, s32[16384]{0:T(1024)S(1)} %bitcast_clamp_fusion), kind=kCustom, calls=%fused_computation | custom fusion | bytes 2162688 | tf_op jit(solution)/shard_map/gather | solution.py:99
  69.7 5.2 copy.68
  77.6 2.6 copy.63
  80.2 3.3 rev.26
  88.1 4.7 multiply_add_fusion
  95.5 3.3 fusion.63
  105.1 41.3 %all_gather.9 = f32[16,3,16,256]{3,2,1,0:T(8,128)S(1)} all-gather(f32[1,3,16,256]{3,2,1,0:T(8,128)S(1)} %pad_maximum_fusion.5), channel_id=1, replica_groups=mesh['fsdp'=32,'ctx'=16] {'ctx'}, dimensions={0}, use_global_device_ids=true | all-gather | bytes 835584 | tf_op jit(solution)/shard_map/all_gather | solution.py:69
  154.1 132.3 %while.38 = (s32[]{:T(128)}, f32[16,16,16]{0,2,1:T(8,128)S(1)}, f32[16,16,16]{0,2,1:T(8,128)}, f32[16,16]{0,1:T(8,128)}, f32[16,16]{0,1:T(8,128)}, /*index=5*/f3...) while((s32[]{:T(128)}, f32[16,16,16]{0,2,1:T(8,128)S(1)}, ...), condition=%wide.region_4.5_spmd.clone, body=%wide.region_1.0_spmd.clone.sunk | while | flops 101380864 | bytes 5014714 | solution.py:121
  156.9 2.9 convolution_bitcast_fusion.8
  162.7 4.5 dynamic_update_slice.17
  172.1 2.9 convolution_bitcast_fusion.8
  179.5 4.5 dynamic_update_slice.17
  188.8 2.9 convolution_bitcast_fusion.8
  196.2 4.5 dynamic_update_slice.17
  205.6 2.9 convolution_bitcast_fusion.8
  213.0 4.5 dynamic_update_slice.17
  222.3 2.9 convolution_bitcast_fusion.8
  229.7 4.5 dynamic_update_slice.17
  239.1 2.9 convolution_bitcast_fusion.8
  246.4 4.5 dynamic_update_slice.17
  255.8 2.9 convolution_bitcast_fusion.8
  263.2 4.5 dynamic_update_slice.17
  272.5 2.9 convolution_bitcast_fusion.8
  279.9 4.5 dynamic_update_slice.17
  286.5 5.8 %rev.30 = f32[16,128,128]{2,1,0:T(8,128)} reverse(f32[16,128,128]{2,1,0:T(8,128)S(1)} %get-tuple-element.242), dimensions={2} | reverse | bytes 2097152 | tf_op jit(solution)/shard_map/jit(_flip)/rev | solution.py:18
  296.5 6.3 %reshape.172 = f32[16,128,255]{2,1,0:T(8,128)} reshape(f32[16,32640]{1,0:T(8,128)} %slice.116) | data formatting | bytes 4177920 | tf_op jit(solution)/shard_map/reshape | solution.py:23
  302.7 2.4 reduce_sum.121
  308.1 2.6 fusion.68
  311.5 32.1 %all-gather = f32[32,16,16]{2,1,0:T(8,128)S(1)} all-gather(f32[2,16,16]{2,1,0:T(8,128)S(1)} %pad_maximum_fusion.6), channel_id=2, replica_groups=mesh['fsdp'=32,'ctx'=16] {'ctx'}, dimensions={0}, use_global_device_ids=true | all-gather | bytes 34816 | tf_op jit(solution)/shard_map/all_gather | solution.py:168
  344.3 5.5 %rev.29 = f32[16,16,1024]{2,1,0:T(8,128)} reverse(f32[16,16,1024]{2,1,0:T(8,128)} %get-tuple-element.493), dimensions={2} | reverse | bytes 2097152 | tf_op jit(solution)/shard_map/jit(_flip)/rev | solution.py:150
  349.8 102.0 %psum.7 = f32[]{:T(128)} all-reduce(f32[]{:T(128)} %multiply_reduce_fusion.6), channel_id=1, replica_groups=mesh['fsdp'=32,'ctx'=16] {'fsdp'}, use_global_device_ids=true, to_apply=%region_17.18 | all-reduce | flops 1 | bytes 8 | tf_op jit(solution)/shard_map/psum | solution.py:169
  455.3 48.9 %while.39 = (s32[]{:T(128)}, f32[16,16,16]{0,2,1:T(8,128)S(1)}, f32[8,128,16,16]{1,0,3,2:T(8,128)}, f32[16,16,1]{0,1,2:T(8,128)S(1)}, f32[8,128,16,16]{1,3,2,0:T...) while((s32[]{:T(128)}, f32[16,16,16]{0,2,1:T(8,128)S(1)}, ...), condition=%wide.region_7.8_spmd.clone, body=%wide.region_6.7_spmd.clone.sunk | while | flops 62996484 | bytes 2277520 | solution.py:134
  456.5 4.5 dynamic_update_slice.18
  462.6 4.5 dynamic_update_slice.18
  468.7 4.5 dynamic_update_slice.18
  474.9 4.5 dynamic_update_slice.18
  481.0 4.5 dynamic_update_slice.18
  487.1 4.5 dynamic_update_slice.18
  493.2 4.5 dynamic_update_slice.18
  499.4 4.5 dynamic_update_slice.18
  504.2 2.5 reshape.168
  506.8 2.6 fusion.61
  511.1 2.4 reshape.164
  513.5 2.6 fusion.62
  523.0 9.4 %collective-permute-done.1 = f32[3,2,256]{1,2,0:T(8,128)S(1)} collective-permute-done((f32[3,2,256]{1,2,0:T(8,128)S(1)}, f32[3,2,256]{1,2,0:T(8,128)S(1)}, u32[]{:S(2)}, u32[]{:S(2)}) %collective-permute-start.1) | collective-permute-done | bytes 6176 | tf_op jit(solution)/shard_map/ppermute | solution.py:13
  533.9 3.3 fusion.54
  537.2 2.6 copy.86
  (221 shorter events, 140.9 us)
Async XLA Ops:
  2.2 85.9 %collective-permute-start = (bf16[3,2,256]{1,2,0:T(8,128)(2,1)}, bf16[3,2,256]{1,2,0:T(8,128)(2,1)}, u32[]{:S(2)}, u32[]{:S(2)}) collective-permute-start(bf16[3,2,256]{1,2,0:T(8,128)(2,1)} %copy.64), channel_id=1, source_target_pairs={{0,1},{1,2},{2,3},{3,4},{4,5},{5,6},{6,7},{7,8},{8,9},{9,10},{10,1... | collective-permute-start | bytes 9224 | tf_op jit(solution)/shard_map/ppermute | solution.py:13
  10.3 4.0 copy-start.19
  10.3 4.3 copy-start.17
  10.3 3.4 copy-start.30
  77.1 6.4 %copy-start.29 = (f32[3,1,256]{2,1,0:T(1,128)S(1)}, f32[3,1,256]{2,1,0:T(1,128)}, u32[]{:S(2)}) copy-start(f32[3,1,256]{2,1,0:T(1,128)} %get-tuple-element.483) | copy-start | bytes 9220
  77.6 8.0 %copy-start.28 = (f32[16,16]{0,1:T(8,128)S(1)}, f32[16,16]{0,1:T(8,128)}, u32[]{:S(2)}) copy-start(f32[16,16]{0,1:T(8,128)} %get-tuple-element.489) | copy-start | bytes 3076
  83.5 4.6 copy-start.26
  92.8 1.6 copy-start
  92.8 2.6 copy-start.10
  92.8 2.7 copy-start.11
  102.2 49.0 %copy-start.8 = (f32[1024,256]{0,1:T(8,128)}, f32[1024,256]{0,1:T(8,128)S(1)}, u32[]{:S(2)}) copy-start(f32[1024,256]{0,1:T(8,128)S(1)} %convert_multiply_fusion.1) | copy-start | bytes 3145732
  103.7 47.7 %copy-start.15 = (f32[16,16,16]{2,1,0:T(8,128)}, f32[16,16,16]{2,1,0:T(8,128)S(1)}, u32[]{:S(2)}) copy-start(f32[16,16,16]{2,1,0:T(8,128)S(1)} %fusion.75) | copy-start | bytes 49156
  151.0 1.0 copy-start.12
  296.4 10.9 %copy-start.14 = (f32[16,256]{0,1:T(8,128)S(1)}, f32[16,256]{0,1:T(8,128)}, u32[]{:S(2)}) copy-start(f32[16,256]{0,1:T(8,128)} %copy.78) | copy-start | bytes 49156
  296.4 10.9 %copy-start.16 = (f32[16,16,16]{2,1,0:T(8,128)S(1)}, f32[16,16,16]{2,1,0:T(8,128)}, u32[]{:S(2)}) copy-start(f32[16,16,16]{2,1,0:T(8,128)} %copy-done.15) | copy-start | bytes 49156
  296.5 11.6 %copy-start.9 = (f32[1024,256]{0,1:T(8,128)S(1)}, f32[1024,256]{0,1:T(8,128)}, u32[]{:S(2)}) copy-start(f32[1024,256]{0,1:T(8,128)} %copy-done.8) | copy-start | bytes 3145732
  310.7 143.4 %copy-start.20 = (f32[16,16]{1,0:T(8,128)S(1)}, f32[16,16]{1,0:T(8,128)}, u32[]{:S(2)}) copy-start(f32[16,16]{1,0:T(8,128)} %get-tuple-element.758) | copy-start | bytes 3076
  455.3 51.5 %copy-start.22 = (f32[16,256]{1,0:T(8,128)S(1)}, f32[16,256]{1,0:T(8,128)}, u32[]{:S(2)}) copy-start(f32[16,256]{1,0:T(8,128)} %get-tuple-element.414) | copy-start | bytes 49156
  455.3 51.6 %copy-start.21 = (f32[16,16]{1,0:T(8,128)S(1)}, f32[16,16]{1,0:T(8,128)}, u32[]{:S(2)}) copy-start(f32[16,16]{1,0:T(8,128)} %get-tuple-element.758) | copy-start | bytes 3076
  504.2 5.2 copy-start.1
  509.4 4.0 copy-start.18
  513.5 4.6 copy-start.2
  513.5 4.6 copy-start.4
  518.1 1.0 copy-start.6
  518.1 2.5 copy-start.23
  518.1 3.9 copy-start.13
  518.1 14.3 %copy-start.3 = (f32[1,1024,256]{1,2,0:T(8,128)S(1)}, f32[1,1024,256]{1,2,0:T(8,128)}, u32[]{:S(2)}) copy-start(f32[1,1024,256]{1,2,0:T(8,128)} %get-tuple-element.471) | copy-start | bytes 3145732
  518.1 14.3 %copy-start.5 = (f32[1,1024,256]{1,2,0:T(8,128)S(1)}, f32[1,1024,256]{1,2,0:T(8,128)}, u32[]{:S(2)}) copy-start(f32[1,1024,256]{1,2,0:T(8,128)} %get-tuple-element.472) | copy-start | bytes 3145732
  519.2 13.2 %collective-permute-start.1 = (f32[3,2,256]{1,2,0:T(8,128)S(1)}, f32[3,2,256]{1,2,0:T(8,128)S(1)}, u32[]{:S(2)}, u32[]{:S(2)}) collective-permute-start(f32[3,2,256]{1,2,0:T(8,128)S(1)} %slice.113), channel_id=1, source_target_pairs={{1,0},{2,1},{3,2},{4,3},{5,4},{6,5},{7,6},{8,7},{9,8},{10,9},{11,1... | collective-permute-start | bytes 18440 | tf_op jit(solution)/shard_map/ppermute | solution.py:13
  523.0 10.9 %copy-start.7 = (f32[1,1024,256]{1,2,0:T(8,128)S(1)}, f32[1,1024,256]{1,2,0:T(8,128)}, u32[]{:S(2)}) copy-start(f32[1,1024,256]{1,2,0:T(8,128)} %copy-done.6) | copy-start | bytes 3145732
  523.0 10.9 %copy-start.24 = (f32[3,256]{1,0:T(4,128)S(1)}, f32[3,256]{1,0:T(4,128)}, u32[]{:S(2)}) copy-start(f32[3,256]{1,0:T(4,128)} %get-tuple-element.499) | copy-start | bytes 9220
  523.0 10.9 %copy-start.25 = (f32[3,256]{1,0:T(4,128)S(1)}, f32[3,256]{1,0:T(4,128)}, u32[]{:S(2)}) copy-start(f32[3,256]{1,0:T(4,128)} %get-tuple-element.500) | copy-start | bytes 9220
  523.0 10.9 %copy-start.27 = (f32[3,1,256]{2,0,1:T(4,128)S(1)}, f32[3,1,256]{2,0,1:T(4,128)}, u32[]{:S(2)}) copy-start(f32[3,1,256]{2,0,1:T(4,128)} %copy-done.26) | copy-start | bytes 9220
